TPU v7x, 128 devices: a whole 4x4x4 slice. The times are simulated.
128 devices in a mesh: lon: 16 (over z_hi, x, core), lat: 8 (over y, z_lo).
Axes of the slice: x: 4, y: 4, z: 4 (z_hi: 2, z_lo: 2; z = z_hi * 2 + z_lo), core: 2. Of those that a mesh axis runs over, the one named last changes fastest.
Arguments:
- state: float32 [75, 4, 128, 2048], P(None, None, 'lat', 'lon'), may hold values from -6 to 6
- depth_levels: int32 [128, 2048], P('lat', 'lon'), may hold values from 0 to 75, as said below
Outputs:
- new_state: float32 [75, 4, 128, 2048], P(None, None, 'lat', 'lon')
Inputs may be any that keep to these rules, and one draw needn't show every extreme that they name: `depth_levels`: the number of wet levels of each column; land (0) grows more common eastward.
All inputs are finite; a program needn't handle non-finite values.
Results may differ from a plain program's by a relative error of at most 0.000059.
Values sent between devices are 32-bit elements; how exact they have to be, the bound alone decides.
A program may use at most 192 MiB of HBM per device.

v0:
```python
import functools

import jax
import jax.numpy as jnp
from jax import lax
from jax.experimental import pallas as pl
from jax.experimental.pallas import tpu as pltpu
from jax.sharding import PartitionSpec as P

MESH = pl.DeviceIdType.MESH
F32 = jnp.float32
MIX = 64.0
ADV = 0.25
SPR = 0.15
PAD = 8


def kernel(nlon, nlat, nz, x, dep, out,
           st1, st2, vf, pb, ob, dpad, dm, tab,
           xc, g1, g2, pe, ve, xe, xe2, gd, dge, dce,
           cw, ce, hw, he,
           lsem, ssem, rsem, csem, crsem, dsem, bsem):
    rows = x.shape[2]
    half = rows // 8
    lon, lat = lax.axis_index("lon"), lax.axis_index("lat")
    west, east = (lax.rem(lon + nlon - 1, nlon), lat), (lax.rem(lon + 1, nlon), lat)
    north, south, mirror = (lon, lat + 1), (lon, lat - 1), (nlon - 1 - lon, lat)
    top, bottom = lat == nlat - 1, lat == 0
    lane = lax.broadcasted_iota(jnp.int32, (8, 128), 1)
    sub = lax.broadcasted_iota(jnp.int32, (8, 128), 0)
    lo = sub < 4

    barrier = pltpu.get_barrier_semaphore()

    def greet(device):
        pl.semaphore_signal(barrier, inc=1, device_id=device, device_id_type=MESH)

    greet(west)
    greet(east)

    @pl.when(jnp.logical_not(top))
    def _():
        greet(north)

    @pl.when(top)
    def _():
        greet(mirror)

    @pl.when(jnp.logical_not(bottom))
    def _():
        greet(south)

    def load(i, src, dst):
        return pltpu.make_async_copy(src, dst, lsem.at[i])

    loads = [
        load(0, x, st1.at[:, :, PAD:PAD + rows, :]),
        load(1, dep, dpad.at[PAD:PAD + rows, :]),
        load(2, x.at[:, :, 0, :], xc.at[:, 0:4, :]),
        load(3, x.at[:, :, rows - 1, :], xc.at[:, 4:8, :]),
    ]
    for one in loads:
        one.start()

    @pl.when(bottom)
    def _():
        pl.semaphore_wait(barrier, 3)

    @pl.when(jnp.logical_not(bottom))
    def _():
        pl.semaphore_wait(barrier, 4)

    def along_lat(step, south_row, north_row, ghost, slot):
        base = 4 * step

        def copy(src, dst, i, device):
            return pltpu.make_async_remote_copy(src, dst, ssem.at[base + i], rsem.at[base + i], device_id=device, device_id_type=MESH)

        up = copy(north_row, ghost(0), slot, north)
        over = copy(north_row, ghost(1), slot + 1, mirror)
        down = copy(south_row, ghost(1), slot + 1, south)
        return up, over, down

    def start_lat(up, over, down):
        @pl.when(jnp.logical_not(top))
        def _():
            up.start()

        @pl.when(top)
        def _():
            over.start()

        @pl.when(jnp.logical_not(bottom))
        def _():
            down.start()

    def recv_lat(up, over, down):
        @pl.when(jnp.logical_not(bottom))
        def _():
            up.wait_recv()

        down.wait_recv()

    def sent_lat(up, over, down):
        @pl.when(jnp.logical_not(top))
        def _():
            up.wait_send()

        @pl.when(top)
        def _():
            over.wait_send()

        @pl.when(jnp.logical_not(bottom))
        def _():
            down.wait_send()

    def ghost_in(buf):
        return lambda e: buf.at[:, 4 * e:4 * e + 4, :]

    lat_depth = along_lat(0, dep.at[0:1, :], dep.at[rows - 1:rows, :], lambda e: gd.at[e], 2)
    lat_1 = along_lat(0, x.at[:, :, 0, :], x.at[:, :, rows - 1, :], ghost_in(g1), 0)
    lat_2 = along_lat(1, xe.at[:, 0:4, :], xe.at[:, 4:8, :], ghost_in(g2), 0)
    start_lat(*lat_depth)
    start_lat(*lat_1)

    zero = jnp.zeros((8, 128), F32)

    @pl.when(bottom)
    def _():
        gd[0] = jnp.zeros_like(gd[0])

        def clear(k, c):
            g1[k, 0:4] = zero[0:4]
            g2[k, 0:4] = zero[0:4]
            return c

        lax.fori_loop(0, nz, clear, 0)

    def clear_pads(k, c):
        for ch in range(4):
            for st in (st1, st2):
                st[k, ch, 0:PAD, :] = zero
                st[k, ch, PAD + rows:PAD + rows + 8, :] = zero
        return c

    lax.fori_loop(0, nz, clear_pads, 0)

    def pivots(k, upper):
        pivot = jnp.where(k == 0, 1.0 + MIX, 1.0 + 2.0 * MIX - MIX * upper)
        inv = 1.0 / pivot
        tab[0, k] = inv
        tab[1, k] = 1.0 / (pivot - MIX)
        tab[2, k] = MIX * inv
        return MIX * inv

    lax.fori_loop(0, nz, pivots, zero)

    def pack(st, depth_too):
        def body(k, acc):
            acc = list(acc)
            here = lane == k
            for ch in range(4):
                for h in range(half):
                    v = st[k, ch, pl.ds(PAD + 8 * h, 8), :]
                    i = ch * half + h
                    acc[i] = jnp.where(here, pltpu.roll(v, k, 1), acc[i])
                    i += 4 * half
                    acc[i] = jnp.where(here, pltpu.roll(v, k + 1, 1), acc[i])
            return tuple(acc)

        acc = list(lax.fori_loop(0, nz, body, (zero,) * (8 * half)))
        if depth_too:
            for h in range(half):
                d = dpad[pl.ds(PAD + 8 * h, 8), :].astype(F32)
                acc[h] = jnp.where(lane == nz, pltpu.roll(d, nz, 1), acc[h])
                i = 4 * half + h
                acc[i] = jnp.where(lane == nz, pltpu.roll(d, nz + 1, 1), acc[i])
        return acc

    def lon_copies(step):
        def copy(src, dst, i, device):
            return pltpu.make_async_remote_copy(src, dst, csem.at[2 * step + i], crsem.at[2 * step + i], device_id=device, device_id_type=MESH)

        return [copy(cw.at[step], he.at[step], 0, west), copy(ce.at[step], hw.at[step], 1, east)]

    def send_lon(step, acc):
        for ch in range(4):
            for h in range(half):
                i = ch * half + h
                cw[step, ch, pl.ds(8 * h, 8), :] = acc[i]
                ce[step, ch, pl.ds(8 * h, 8), :] = acc[4 * half + i]
        copies = lon_copies(step)
        for one in copies:
            one.start()
        return copies

    loads[1].wait()
    dpad[0:PAD, :] = jnp.zeros((8, 128), jnp.int32)
    dpad[PAD + rows:PAD + rows + 8, :] = jnp.zeros((8, 128), jnp.int32)
    loads[0].wait()
    lon_1 = send_lon(0, pack(st1, True))

    def shifted(v, west_halo, east_halo, k):
        from_east = jnp.where(lane == 127, pltpu.roll(east_halo, 127 - k, 1), pltpu.roll(v, 127, 1))
        from_west = jnp.where(lane == 0, pltpu.roll(west_halo, lax.rem(128 - k, 128), 1), pltpu.roll(v, 1, 1))
        return from_east, from_west

    def depth_maps():
        for h in range(half):
            d = dpad[pl.ds(PAD + 8 * h, 8), :].astype(F32)
            e, w = shifted(d, hw[0, 0, pl.ds(8 * h, 8), :], he[0, 0, pl.ds(8 * h, 8), :], nz)
            at = pl.ds(8 * h, 8)
            dm[0, at, :] = d.astype(jnp.int32)
            dm[1, at, :] = e.astype(jnp.int32)
            dm[2, at, :] = w.astype(jnp.int32)
            dm[3, at, :] = dpad[pl.ds(PAD + 8 * h + 1, 8), :]
            dm[4, at, :] = dpad[pl.ds(PAD + 8 * h - 1, 8), :]

    total = F32(rows * nlat)

    def rotation(h):
        row = (sub + (8 * h + lat * rows)).astype(F32)
        return 0.1 + 0.4 * (row + 0.5) / total

    def main(st, step, dst, dst_row):
        def forward(k, carry):
            prev = list(carry[0:4 * half])
            grad_e = list(carry[4 * half:5 * half])
            grad_n = list(carry[5 * half:6 * half])
            inv_in, inv_low = tab[0, k], tab[1, k]
            for h in range(half):
                at = pl.ds(8 * h, 8)
                wet = []
                for i in range(5):
                    wet.append(k < dm[i, at, :])
                w15 = [jnp.where(m, F32(SPR), F32(0.0)) for m in wet[1:]]
                q, qe, qw, qn, qs = [], [], [], [], []
                for ch in range(4):
                    v = st[k, ch, pl.ds(PAD + 8 * h, 8), :]
                    e, w = shifted(v, hw[step, ch, at, :], he[step, ch, at, :], k)
                    q.append(v)
                    qe.append(e)
                    qw.append(w)
                    qn.append(st[k, ch, pl.ds(PAD + 8 * h + 1, 8), :])
                    qs.append(st[k, ch, pl.ds(PAD + 8 * h - 1, 8), :])
                a_e = w15[0] - ADV * qe[2]
                a_w = w15[1] + ADV * qw[2]
                a_n = w15[2] - ADV * qn[3]
                a_s = w15[3] + ADV * qs[3]
                centre = 1.0 - (w15[0] + w15[1]) - (w15[2] + w15[3])

                def dense(p, m):
                    return jnp.where(m, 0.75 * p[1] - 0.25 * p[0], 0.0)

                grad_e[h] = grad_e[h] + (dense(qe, wet[1]) - dense(qw, wet[2]))
                grad_n[h] = grad_n[h] + (dense(qn, wet[3]) - dense(qs, wet[4]))
                turn = rotation(h)
                low = (k + 1) == dm[0, at, :]
                inv = jnp.where(low, inv_low, inv_in)
                for ch in range(4):
                    p = (centre * q[ch] + a_e * qe[ch]) + (a_w * qw[ch] + a_n * qn[ch]) + a_s * qs[ch]
                    if ch == 2:
                        p = p + (turn * q[3] - 0.1 * grad_e[h])
                    if ch == 3:
                        p = p - (turn * q[2] + 0.1 * grad_n[h])
                    pb[k, ch, at, :] = p
                    i = ch * half + h
                    prev[i] = jnp.where(wet[0], (p - MIX * prev[i]) * inv, 0.0)
                    vf[k, ch, at, :] = prev[i]
            return tuple(prev + grad_e + grad_n)

        lax.fori_loop(0, nz, forward, (zero,) * (6 * half))

        copies = [pltpu.make_async_copy(pb.at[:, :, 0, :], pe.at[:, 0:4, :], dsem.at[0]),
                  pltpu.make_async_copy(pb.at[:, :, rows - 1, :], pe.at[:, 4:8, :], dsem.at[1])]
        for one in copies:
            one.start()

        def backward(j, carry):
            k = nz - 1 - j
            up = tab[2, k]
            new = []
            for ch in range(4):
                for h in range(half):
                    s = vf[k, ch, pl.ds(8 * h, 8), :] - up * carry[ch * half + h]
                    dst[k, ch, pl.ds(dst_row + 8 * h, 8), :] = s
                    new.append(s)
            return tuple(new)

        lax.fori_loop(0, nz, backward, (zero,) * (4 * half))
        for one in copies:
            one.wait()

    flip = jnp.logical_and(top, sub >= 4)
    index = jnp.where(flip, 127 - lane, lane)
    sign = jnp.where(jnp.logical_and(flip, lax.rem(sub, 4) >= 2), F32(-1.0), F32(1.0))
    slope = jnp.where(lo, F32(ADV), jnp.where(top, F32(ADV), F32(-ADV)))
    push = jnp.where(sub == 3, F32(0.1), jnp.where(sub == 7, F32(-0.1), F32(0.0)))

    def mirrored(v):
        return jnp.take_along_axis(v, index, axis=1)

    def edges(ghost, centre, solved):
        def both(k, c):
            return mirrored(jnp.where(lo, ghost[k, c:c + 1, :], ghost[k, c + 4:c + 5, :]))

        def forward(k, carry):
            prev, grad = carry
            g = mirrored(ghost[k])
            warm, salt, vel = both(k, 0), both(k, 1), both(k, 3)
            wet = k < dge[...]
            w15 = jnp.where(wet, F32(SPR), 0.0)
            grad = grad + push * jnp.where(wet, 0.75 * salt - 0.25 * warm, 0.0)
            p = pe[k] + ((w15 + slope * vel) * (sign * g) - w15 * centre[k]) + grad
            depth = dce[...]
            inv = jnp.where((k + 1) == depth, tab[1, k], tab[0, k])
            prev = jnp.where(k < depth, (p - MIX * prev) * inv, 0.0)
            ve[k] = prev
            return prev, grad

        lax.fori_loop(0, nz, forward, (zero, zero))

        def backward(j, s):
            k = nz - 1 - j
            s = ve[k] - tab[2, k] * s
            solved[k] = s
            return s

        lax.fori_loop(0, nz, backward, zero)

    for one in lon_1:
        one.wait_recv()
    depth_maps()
    main(st1, 0, st2, PAD)

    loads[2].wait()
    loads[3].wait()
    recv_lat(*lat_depth)
    dce[...] = jnp.where(lo, dm[0, 0:1, :], dm[0, rows - 1:rows, :])
    dge[...] = mirrored(jnp.where(lo, gd[0], gd[1]).astype(F32)).astype(jnp.int32)
    recv_lat(*lat_1)
    edges(g1, xc, xe)
    start_lat(*lat_2)
    patch = [pltpu.make_async_copy(xe.at[:, 0:4, :], st2.at[:, :, PAD, :], bsem.at[0]),
             pltpu.make_async_copy(xe.at[:, 4:8, :], st2.at[:, :, PAD + rows - 1, :], bsem.at[1])]
    for one in patch:
        one.start()
    for one in patch:
        one.wait()
    lon_2 = send_lon(1, pack(st2, False))
    for one in lon_2:
        one.wait_recv()
    main(st2, 1, ob, 0)
    whole = pltpu.make_async_copy(ob, out, bsem.at[2])
    whole.start()
    recv_lat(*lat_2)
    edges(g2, xe, xe2)
    whole.wait()
    last = [pltpu.make_async_copy(xe2.at[:, 0:4, :], out.at[:, :, 0, :], bsem.at[0]),
            pltpu.make_async_copy(xe2.at[:, 4:8, :], out.at[:, :, rows - 1, :], bsem.at[1])]
    for one in last:
        one.start()
    for one in lon_1 + lon_2:
        one.wait_send()
    sent_lat(*lat_depth)
    sent_lat(*lat_1)
    sent_lat(*lat_2)
    for one in last:
        one.wait()


def solution(mesh):
    nlon, nlat = mesh.shape["lon"], mesh.shape["lat"]

    def on_device(state, depth_levels):
        nz, _, rows, cols = state.shape
        edge = pltpu.VMEM((nz, 8, cols), F32)
        dma = pltpu.SemaphoreType.DMA
        return pl.pallas_call(
            functools.partial(kernel, nlon, nlat, nz),
            out_shape=jax.ShapeDtypeStruct(state.shape, F32),
            in_specs=[pl.BlockSpec(memory_space=pl.ANY)] * 2,
            out_specs=pl.BlockSpec(memory_space=pl.ANY),
            scratch_shapes=[
                pltpu.VMEM((nz, 4, rows + 16, cols), F32),
                pltpu.VMEM((nz, 4, rows + 16, cols), F32),
                pltpu.VMEM((nz, 4, rows, cols), F32),
                pltpu.VMEM((nz, 4, rows, cols), F32),
                pltpu.VMEM((nz, 4, rows, cols), F32),
                pltpu.VMEM((rows + 16, cols), jnp.int32),
                pltpu.VMEM((5, rows, cols), jnp.int32),
                pltpu.VMEM((3, nz, 8, cols), F32),
                edge, edge, edge, edge, edge, edge, edge,
                pltpu.VMEM((2, 1, cols), jnp.int32),
                pltpu.VMEM((8, cols), jnp.int32),
                pltpu.VMEM((8, cols), jnp.int32),
                pltpu.VMEM((2, 4, rows, cols), F32),
                pltpu.VMEM((2, 4, rows, cols), F32),
                pltpu.VMEM((2, 4, rows, cols), F32),
                pltpu.VMEM((2, 4, rows, cols), F32),
                dma((4,)), dma((8,)), dma((8,)), dma((4,)), dma((4,)), dma((2,)), dma((3,)),
            ],
            compiler_params=pltpu.CompilerParams(
                collective_id=0, has_side_effects=True, vmem_limit_bytes=48 << 20
            ),
        )(state, depth_levels)

    return jax.shard_map(
        on_device,
        mesh=mesh,
        in_specs=(P(None, None, "lat", "lon"), P("lat", "lon")),
        out_specs=P(None, None, "lat", "lon"),
        check_vma=False,
    )
```

profile of v0, /device:TPU:0, one launch (start us, length us, event | category | flops | bytes accessed | tf_op | source)
XLA Modules:
  0.0 64.6 jit_solution(4028201001027801658)
XLA Ops:
  0.0 0.0 copy-start
  0.0 1.7 %copy-done = f32[75,4,16,128]{3,2,1,0:T(8,128)S(1)} copy-done((f32[75,4,16,128]{3,2,1,0:T(8,128)S(1)}, f32[75,4,16,128]{3,2,1,0:T(8,128)}, u32[]{:S(2)}) %copy-start) | copy-done | bytes 2457624
  1.7 0.0 copy-start.1
  1.7 0.7 %copy-done.1 = s32[16,128]{1,0:T(8,128)S(1)} copy-done((s32[16,128]{1,0:T(8,128)S(1)}, s32[16,128]{1,0:T(8,128)}, u32[]{:S(2)}) %copy-start.1) | copy-done | bytes 8216
  2.4 60.7 %shard_map.28 = f32[75,4,16,128]{3,2,1,0:T(8,128)S(1)} custom-call(f32[75,4,16,128]{3,2,1,0:T(8,128)S(1)} %copy-done, s32[16,128]{1,0:T(8,128)S(1)} %copy-done.1), custom_call_target="tpu_custom_call" | custom-call | tf_op jit(solution)/shard_map/pallas_call | solution.py:379
  63.1 1.4 %copy.4 = f32[75,4,16,128]{3,2,1,0:T(8,128)} copy(f32[75,4,16,128]{3,2,1,0:T(8,128)S(1)} %shard_map.28) | data formatting | bytes 4915200
Async XLA Ops:
  0.0 1.7 %copy-start = (f32[75,4,16,128]{3,2,1,0:T(8,128)S(1)}, f32[75,4,16,128]{3,2,1,0:T(8,128)}, u32[]{:S(2)}) copy-start(f32[75,4,16,128]{3,2,1,0:T(8,128)} %x.1) | copy-start | bytes 7372804
  1.7 0.7 %copy-start.1 = (s32[16,128]{1,0:T(8,128)S(1)}, s32[16,128]{1,0:T(8,128)}, u32[]{:S(2)}) copy-start(s32[16,128]{1,0:T(8,128)} %dep.1) | copy-start | bytes 24580
where the time goes:
time: 64.7 us; the launch traced here: 64.6 us
  Pallas kernels  60.7 us (94%)
  local copies, waits for them, and re-layouts  3.83 us (6%)
    pallas_call x1, Pallas kernels, on_device(): pl.pallas_call(functools.partial(kernel, nlon, nlat, nz), out_shape=jax.S...  60.7 us
    unnamed x5, local copies, waits for them, and re-layouts  3.83 us

commit v1 on v0

--- a/solution.py
+++ b/solution.py
@@ -16,7 +16,7 @@
 
 
 def kernel(nlon, nlat, nz, x, dep, out,
-           st1, st2, vf, pb, ob, dpad, dm, tab,
+           st1, st2, vf, pb, dpad, dm, tab,
            xc, g1, g2, pe, ve, xe, xe2, gd, dge, dce,
            cw, ce, hw, he,
            lsem, ssem, rsem, csem, crsem, dsem, bsem):
@@ -134,7 +134,7 @@
             g2[k, 0:4] = zero[0:4]
             return c
 
-        lax.fori_loop(0, nz, clear, 0)
+        lax.fori_loop(0, nz, clear, 0, unroll=5)
 
     def clear_pads(k, c):
         for ch in range(4):
@@ -143,7 +143,7 @@
                 st[k, ch, PAD + rows:PAD + rows + 8, :] = zero
         return c
 
-    lax.fori_loop(0, nz, clear_pads, 0)
+    lax.fori_loop(0, nz, clear_pads, 0, unroll=5)
 
     def pivots(k, upper):
         pivot = jnp.where(k == 0, 1.0 + MIX, 1.0 + 2.0 * MIX - MIX * upper)
@@ -153,7 +153,7 @@
         tab[2, k] = MIX * inv
         return MIX * inv
 
-    lax.fori_loop(0, nz, pivots, zero)
+    lax.fori_loop(0, nz, pivots, zero, unroll=5)
 
     def pack(st, depth_too):
         def body(k, acc):
@@ -168,7 +168,7 @@
                     acc[i] = jnp.where(here, pltpu.roll(v, k + 1, 1), acc[i])
             return tuple(acc)
 
-        acc = list(lax.fori_loop(0, nz, body, (zero,) * (8 * half)))
+        acc = list(lax.fori_loop(0, nz, body, (zero,) * (8 * half), unroll=15))
         if depth_too:
             for h in range(half):
                 d = dpad[pl.ds(PAD + 8 * h, 8), :].astype(F32)
@@ -269,7 +269,7 @@
                     vf[k, ch, at, :] = prev[i]
             return tuple(prev + grad_e + grad_n)
 
-        lax.fori_loop(0, nz, forward, (zero,) * (6 * half))
+        lax.fori_loop(0, nz, forward, (zero,) * (6 * half), unroll=5)
 
         copies = [pltpu.make_async_copy(pb.at[:, :, 0, :], pe.at[:, 0:4, :], dsem.at[0]),
                   pltpu.make_async_copy(pb.at[:, :, rows - 1, :], pe.at[:, 4:8, :], dsem.at[1])]
@@ -287,7 +287,7 @@
                     new.append(s)
             return tuple(new)
 
-        lax.fori_loop(0, nz, backward, (zero,) * (4 * half))
+        lax.fori_loop(0, nz, backward, (zero,) * (4 * half), unroll=15)
         for one in copies:
             one.wait()
 
@@ -318,7 +318,7 @@
             ve[k] = prev
             return prev, grad
 
-        lax.fori_loop(0, nz, forward, (zero, zero))
+        lax.fori_loop(0, nz, forward, (zero, zero), unroll=25)
 
         def backward(j, s):
             k = nz - 1 - j
@@ -326,7 +326,7 @@
             solved[k] = s
             return s
 
-        lax.fori_loop(0, nz, backward, zero)
+        lax.fori_loop(0, nz, backward, zero, unroll=25)
 
     for one in lon_1:
         one.wait_recv()
@@ -350,12 +350,9 @@
     lon_2 = send_lon(1, pack(st2, False))
     for one in lon_2:
         one.wait_recv()
-    main(st2, 1, ob, 0)
-    whole = pltpu.make_async_copy(ob, out, bsem.at[2])
-    whole.start()
+    main(st2, 1, out, 0)
     recv_lat(*lat_2)
     edges(g2, xe, xe2)
-    whole.wait()
     last = [pltpu.make_async_copy(xe2.at[:, 0:4, :], out.at[:, :, 0, :], bsem.at[0]),
             pltpu.make_async_copy(xe2.at[:, 4:8, :], out.at[:, :, rows - 1, :], bsem.at[1])]
     for one in last:
@@ -379,12 +376,11 @@
         return pl.pallas_call(
             functools.partial(kernel, nlon, nlat, nz),
             out_shape=jax.ShapeDtypeStruct(state.shape, F32),
-            in_specs=[pl.BlockSpec(memory_space=pl.ANY)] * 2,
-            out_specs=pl.BlockSpec(memory_space=pl.ANY),
+            in_specs=[pl.BlockSpec(memory_space=pltpu.HBM)] * 2,
+            out_specs=pl.BlockSpec(memory_space=pltpu.VMEM),
             scratch_shapes=[
                 pltpu.VMEM((nz, 4, rows + 16, cols), F32),
                 pltpu.VMEM((nz, 4, rows + 16, cols), F32),
-                pltpu.VMEM((nz, 4, rows, cols), F32),
                 pltpu.VMEM((nz, 4, rows, cols), F32),
                 pltpu.VMEM((nz, 4, rows, cols), F32),
                 pltpu.VMEM((rows + 16, cols), jnp.int32),
@@ -398,7 +394,7 @@
                 pltpu.VMEM((2, 4, rows, cols), F32),
                 pltpu.VMEM((2, 4, rows, cols), F32),
                 pltpu.VMEM((2, 4, rows, cols), F32),
-                dma((4,)), dma((8,)), dma((8,)), dma((4,)), dma((4,)), dma((2,)), dma((3,)),
+                dma((4,)), dma((8,)), dma((8,)), dma((4,)), dma((4,)), dma((2,)), dma((2,)),
             ],
             compiler_params=pltpu.CompilerParams(
                 collective_id=0, has_side_effects=True, vmem_limit_bytes=48 << 20

time: 64.7 us -> 33.8 us (0.52)
  the two profiles are of different devices: /device:TPU:0 before, /device:TPU:16 now
where the time goes in v1:
time: 33.8 us; the launch traced here: 33.6 us
  Pallas kernels  29.8 us (88%)
  local copies, waits for them, and re-layouts  3.83 us (11%)
    pallas_call x1, Pallas kernels, on_device(): pl.pallas_call(functools.partial(kernel, nlon, nlat, nz), out_shape=jax.S...  29.8 us
    unnamed x5, local copies, waits for them, and re-layouts  3.83 us

profile of v1, /device:TPU:16, one launch (start us, length us, event | category | flops | bytes accessed | tf_op | source)
XLA Modules:
  0.0 33.6 jit_solution(7651473823193066622)
XLA Ops:
  0.0 0.0 copy-start
  0.0 1.7 %copy-done = f32[75,4,16,128]{3,2,1,0:T(8,128)S(1)} copy-done((f32[75,4,16,128]{3,2,1,0:T(8,128)S(1)}, f32[75,4,16,128]{3,2,1,0:T(8,128)}, u32[]{:S(2)}) %copy-start) | copy-done | bytes 2457624
  1.7 0.0 copy-start.1
  1.7 0.7 %copy-done.1 = s32[16,128]{1,0:T(8,128)S(1)} copy-done((s32[16,128]{1,0:T(8,128)S(1)}, s32[16,128]{1,0:T(8,128)}, u32[]{:S(2)}) %copy-start.1) | copy-done | bytes 8216
  2.4 29.8 %shard_map.28 = f32[75,4,16,128]{3,2,1,0:T(8,128)S(1)} custom-call(f32[75,4,16,128]{3,2,1,0:T(8,128)S(1)} %copy-done, s32[16,128]{1,0:T(8,128)S(1)} %copy-done.1), custom_call_target="tpu_custom_call" | custom-call | tf_op jit(solution)/shard_map/pallas_call | solution.py:376
  32.2 1.4 %copy.4 = f32[75,4,16,128]{3,2,1,0:T(8,128)} copy(f32[75,4,16,128]{3,2,1,0:T(8,128)S(1)} %shard_map.28) | data formatting | bytes 4915200
Async XLA Ops:
  0.0 1.7 %copy-start = (f32[75,4,16,128]{3,2,1,0:T(8,128)S(1)}, f32[75,4,16,128]{3,2,1,0:T(8,128)}, u32[]{:S(2)}) copy-start(f32[75,4,16,128]{3,2,1,0:T(8,128)} %x.1) | copy-start | bytes 7372804
  1.7 0.7 %copy-start.1 = (s32[16,128]{1,0:T(8,128)S(1)}, s32[16,128]{1,0:T(8,128)}, u32[]{:S(2)}) copy-start(s32[16,128]{1,0:T(8,128)} %dep.1) | copy-start | bytes 24580

commit v2 on v1

--- a/solution.py
+++ b/solution.py
@@ -17,15 +17,16 @@
 
 def kernel(nlon, nlat, nz, x, dep, out,
            st1, st2, vf, pb, dpad, dm, tab,
-           xc, g1, g2, pe, ve, xe, xe2, gd, dge, dce,
-           cw, ce, hw, he,
+           xc, g1, g2, pe, ve, xe, xe2, h1, h2, hd, gd, dge, dce,
+           cw, ce, hw, he, ca,
            lsem, ssem, rsem, csem, crsem, dsem, bsem):
     rows = x.shape[2]
     half = rows // 8
     lon, lat = lax.axis_index("lon"), lax.axis_index("lat")
     west, east = (lax.rem(lon + nlon - 1, nlon), lat), (lax.rem(lon + 1, nlon), lat)
-    north, south, mirror = (lon, lat + 1), (lon, lat - 1), (nlon - 1 - lon, lat)
-    top, bottom = lat == nlat - 1, lat == 0
+    north, south = (lon, lat + 1), (lon, lat - 1)
+    top, near, bottom = lat == nlat - 1, lat == nlat - 2, lat == 0
+    over_south, over_north = (nlon - 1 - lon, lat - 1), (nlon - 1 - lon, lat + 1)
     lane = lax.broadcasted_iota(jnp.int32, (8, 128), 1)
     sub = lax.broadcasted_iota(jnp.int32, (8, 128), 0)
     lo = sub < 4
@@ -44,7 +45,11 @@
 
     @pl.when(top)
     def _():
-        greet(mirror)
+        greet(over_south)
+
+    @pl.when(near)
+    def _():
+        greet(over_north)
 
     @pl.when(jnp.logical_not(bottom))
     def _():
@@ -66,49 +71,75 @@
     def _():
         pl.semaphore_wait(barrier, 3)
 
-    @pl.when(jnp.logical_not(bottom))
+    @pl.when(near)
+    def _():
+        pl.semaphore_wait(barrier, 5)
+
+    @pl.when(jnp.logical_not(jnp.logical_or(bottom, near)))
     def _():
         pl.semaphore_wait(barrier, 4)
 
-    def along_lat(step, south_row, north_row, ghost, slot):
-        base = 4 * step
-
+    def along_lat(base, south_row, north_row, ghost, held, parts):
         def copy(src, dst, i, device):
-            return pltpu.make_async_remote_copy(src, dst, ssem.at[base + i], rsem.at[base + i], device_id=device, device_id_type=MESH)
-
-        up = copy(north_row, ghost(0), slot, north)
-        over = copy(north_row, ghost(1), slot + 1, mirror)
-        down = copy(south_row, ghost(1), slot + 1, south)
-        return up, over, down
-
-    def start_lat(up, over, down):
+            return pltpu.make_async_remote_copy(src, dst, ssem.at[i], rsem.at[i], device_id=device, device_id_type=MESH)
+
+        up = copy(north_row, ghost(0), base, north)
+        down = copy(south_row, ghost(1), base + 1, south)
+        over, on = [], []
+        for j, (at, size) in enumerate(parts):
+            part = pl.ds(at, size)
+            over.append(copy(north_row.at[part], held.at[part], base + 2 + 2 * j, over_south))
+            on.append(copy(held.at[part], ghost(1).at[part], base + 3 + 2 * j, north))
+        return up, down, over, on
+
+    def start_lat(up, down, over, on):
+        @pl.when(top)
+        def _():
+            for one in over:
+                one.start()
+
         @pl.when(jnp.logical_not(top))
         def _():
             up.start()
 
+        @pl.when(jnp.logical_not(bottom))
+        def _():
+            down.start()
+
+    def relay(lats, j):
+        @pl.when(near)
+        def _():
+            lats[2][j].wait_recv()
+            lats[3][j].start()
+
+    def recv_lat(up, down, over, on):
+        @pl.when(jnp.logical_not(bottom))
+        def _():
+            up.wait_recv()
+
+        @pl.when(jnp.logical_not(top))
+        def _():
+            down.wait_recv()
+
         @pl.when(top)
         def _():
-            over.start()
-
-        @pl.when(jnp.logical_not(bottom))
-        def _():
-            down.start()
-
-    def recv_lat(up, over, down):
-        @pl.when(jnp.logical_not(bottom))
-        def _():
-            up.wait_recv()
-
-        down.wait_recv()
-
-    def sent_lat(up, over, down):
+            for one in on:
+                one.wait_recv()
+
+    def sent_lat(up, down, over, on):
         @pl.when(jnp.logical_not(top))
         def _():
             up.wait_send()
 
         @pl.when(top)
         def _():
-            over.wait_send()
+            for one in over:
+                one.wait_send()
+
+        @pl.when(near)
+        def _():
+            for one in on:
+                one.wait_send()
 
         @pl.when(jnp.logical_not(bottom))
         def _():
@@ -117,9 +148,11 @@
     def ghost_in(buf):
         return lambda e: buf.at[:, 4 * e:4 * e + 4, :]
 
-    lat_depth = along_lat(0, dep.at[0:1, :], dep.at[rows - 1:rows, :], lambda e: gd.at[e], 2)
-    lat_1 = along_lat(0, x.at[:, :, 0, :], x.at[:, :, rows - 1, :], ghost_in(g1), 0)
-    lat_2 = along_lat(1, xe.at[:, 0:4, :], xe.at[:, 4:8, :], ghost_in(g2), 0)
+    third = nz // 3
+    parts = [(0, third), (third, third), (2 * third, nz - 2 * third)]
+    lat_depth = along_lat(0, dep.at[0:1, :], dep.at[rows - 1:rows, :], lambda e: gd.at[e], hd, [(0, 1)])
+    lat_1 = along_lat(4, x.at[:, :, 0, :], x.at[:, :, rows - 1, :], ghost_in(g1), h1, parts)
+    lat_2 = along_lat(12, xe.at[:, 0:4, :], xe.at[:, 4:8, :], ghost_in(g2), h2, parts)
     start_lat(*lat_depth)
     start_lat(*lat_1)
 
@@ -144,16 +177,6 @@
         return c
 
     lax.fori_loop(0, nz, clear_pads, 0, unroll=5)
-
-    def pivots(k, upper):
-        pivot = jnp.where(k == 0, 1.0 + MIX, 1.0 + 2.0 * MIX - MIX * upper)
-        inv = 1.0 / pivot
-        tab[0, k] = inv
-        tab[1, k] = 1.0 / (pivot - MIX)
-        tab[2, k] = MIX * inv
-        return MIX * inv
-
-    lax.fori_loop(0, nz, pivots, zero, unroll=5)
 
     def pack(st, depth_too):
         def body(k, acc):
@@ -200,19 +223,15 @@
     loads[0].wait()
     lon_1 = send_lon(0, pack(st1, True))
 
-    def shifted(v, west_halo, east_halo, k):
-        from_east = jnp.where(lane == 127, pltpu.roll(east_halo, 127 - k, 1), pltpu.roll(v, 127, 1))
-        from_west = jnp.where(lane == 0, pltpu.roll(west_halo, lax.rem(128 - k, 128), 1), pltpu.roll(v, 1, 1))
-        return from_east, from_west
+    first, final = lane == 0, lane == 127
 
     def depth_maps():
         for h in range(half):
-            d = dpad[pl.ds(PAD + 8 * h, 8), :].astype(F32)
-            e, w = shifted(d, hw[0, 0, pl.ds(8 * h, 8), :], he[0, 0, pl.ds(8 * h, 8), :], nz)
             at = pl.ds(8 * h, 8)
-            dm[0, at, :] = d.astype(jnp.int32)
-            dm[1, at, :] = e.astype(jnp.int32)
-            dm[2, at, :] = w.astype(jnp.int32)
+            d = dpad[pl.ds(PAD + 8 * h, 8), :]
+            dm[0, at, :] = d
+            dm[1, at, :] = jnp.where(final, 0, pltpu.roll(d, 127, 1))
+            dm[2, at, :] = jnp.where(first, 0, pltpu.roll(d, 1, 1))
             dm[3, at, :] = dpad[pl.ds(PAD + 8 * h + 1, 8), :]
             dm[4, at, :] = dpad[pl.ds(PAD + 8 * h - 1, 8), :]
 
@@ -222,41 +241,38 @@
         row = (sub + (8 * h + lat * rows)).astype(F32)
         return 0.1 + 0.4 * (row + 0.5) / total
 
-    def main(st, step, dst, dst_row):
-        def forward(k, carry):
-            prev = list(carry[0:4 * half])
-            grad_e = list(carry[4 * half:5 * half])
-            grad_n = list(carry[5 * half:6 * half])
-            inv_in, inv_low = tab[0, k], tab[1, k]
+    def dense(warm, salt, wet):
+        return jnp.where(wet, 0.75 * salt - 0.25 * warm, 0.0)
+
+    def stencil(st, make_table):
+        def body(k, carry):
+            grad_e = list(carry[0:half])
+            grad_n = list(carry[half:2 * half])
+            upper = carry[2 * half]
+            if make_table:
+                pivot = jnp.where(k == 0, 1.0 + MIX, 1.0 + 2.0 * MIX - MIX * upper)
+                inv = 1.0 / pivot
+                upper = MIX * inv
+                tab[0, k] = inv
+                tab[1, k] = 1.0 / (pivot - MIX)
+                tab[2, k] = upper
             for h in range(half):
                 at = pl.ds(8 * h, 8)
-                wet = []
-                for i in range(5):
-                    wet.append(k < dm[i, at, :])
+                wet = [None] + [k < dm[i, at, :] for i in range(1, 5)]
                 w15 = [jnp.where(m, F32(SPR), F32(0.0)) for m in wet[1:]]
-                q, qe, qw, qn, qs = [], [], [], [], []
-                for ch in range(4):
-                    v = st[k, ch, pl.ds(PAD + 8 * h, 8), :]
-                    e, w = shifted(v, hw[step, ch, at, :], he[step, ch, at, :], k)
-                    q.append(v)
-                    qe.append(e)
-                    qw.append(w)
-                    qn.append(st[k, ch, pl.ds(PAD + 8 * h + 1, 8), :])
-                    qs.append(st[k, ch, pl.ds(PAD + 8 * h - 1, 8), :])
-                a_e = w15[0] - ADV * qe[2]
-                a_w = w15[1] + ADV * qw[2]
+                q = [st[k, ch, pl.ds(PAD + 8 * h, 8), :] for ch in range(4)]
+                qe = [pltpu.roll(v, 127, 1) for v in q]
+                qw = [pltpu.roll(v, 1, 1) for v in q]
+                qn = [st[k, ch, pl.ds(PAD + 8 * h + 1, 8), :] for ch in range(4)]
+                qs = [st[k, ch, pl.ds(PAD + 8 * h - 1, 8), :] for ch in range(4)]
+                a_e = jnp.where(final, 0.0, w15[0] - ADV * qe[2])
+                a_w = jnp.where(first, 0.0, w15[1] + ADV * qw[2])
                 a_n = w15[2] - ADV * qn[3]
                 a_s = w15[3] + ADV * qs[3]
                 centre = 1.0 - (w15[0] + w15[1]) - (w15[2] + w15[3])
-
-                def dense(p, m):
-                    return jnp.where(m, 0.75 * p[1] - 0.25 * p[0], 0.0)
-
-                grad_e[h] = grad_e[h] + (dense(qe, wet[1]) - dense(qw, wet[2]))
-                grad_n[h] = grad_n[h] + (dense(qn, wet[3]) - dense(qs, wet[4]))
+                grad_e[h] = grad_e[h] + (dense(qe[0], qe[1], wet[1]) - dense(qw[0], qw[1], wet[2]))
+                grad_n[h] = grad_n[h] + (dense(qn[0], qn[1], wet[3]) - dense(qs[0], qs[1], wet[4]))
                 turn = rotation(h)
-                low = (k + 1) == dm[0, at, :]
-                inv = jnp.where(low, inv_low, inv_in)
                 for ch in range(4):
                     p = (centre * q[ch] + a_e * qe[ch]) + (a_w * qw[ch] + a_n * qn[ch]) + a_s * qs[ch]
                     if ch == 2:
@@ -264,12 +280,62 @@
                     if ch == 3:
                         p = p - (turn * q[2] + 0.1 * grad_n[h])
                     pb[k, ch, at, :] = p
+            return tuple(grad_e + grad_n + [upper])
+
+        lax.fori_loop(0, nz, body, (zero,) * (2 * half + 1), unroll=5)
+
+    def columns(step):
+        for h in range(half):
+            at = pl.ds(8 * h, 8)
+            adds = []
+            for halo, own, way in ((hw, cw, 1.0), (he, ce, -1.0)):
+                deep = jnp.broadcast_to(halo[0, 0, at, nz:nz + 1], (8, 128)).astype(jnp.int32)
+                wet = lane < deep
+                w15 = jnp.where(wet, F32(SPR), F32(0.0))
+                q = [halo[step, ch, at, :] for ch in range(4)]
+                coef = w15 + (way * ADV) * q[2]
+                push = dense(q[0], q[1], wet)
+                shift = 1
+                while shift < nz:
+                    push = push + jnp.where(lane >= shift, pltpu.roll(push, shift, 1), 0.0)
+                    shift *= 2
+                add = [coef * q[ch] - w15 * own[step, ch, at, :] for ch in range(4)]
+                add[2] = add[2] + (way * 0.1) * push
+                adds.append(add)
+            even = lax.rem(lane, 2) == 0
+            for ch in range(4):
+                w, e = adds[0][ch], pltpu.roll(adds[1][ch], 127, 1)
+                ca[0, ch, at, :] = jnp.where(even, w, e)
+                ca[1, ch, at, :] = jnp.where(even, e, w)
+
+    outer = jnp.logical_or(first, final)
+
+    def inverse(k, depth):
+        inv = jnp.where((k + 1) == depth, tab[1, k], tab[0, k])
+        return jnp.where(k < depth, inv, 0.0)
+
+    def sweeps(dst, dst_row, lats):
+        def forward(k, carry):
+            new = list(carry)
+            back = lax.rem(128 - k, 128)
+            odd = lax.rem(k, 2)
+            for h in range(half):
+                at = pl.ds(8 * h, 8)
+                inv = inverse(k, dm[0, at, :])
+                low = MIX * inv
+                for ch in range(4):
+                    p = pb[k, ch, at, :] + jnp.where(outer, pltpu.roll(ca[odd, ch, at, :], back, 1), 0.0)
+                    pb[k, ch, at, :] = p
                     i = ch * half + h
-                    prev[i] = jnp.where(wet[0], (p - MIX * prev[i]) * inv, 0.0)
-                    vf[k, ch, at, :] = prev[i]
-            return tuple(prev + grad_e + grad_n)
-
-        lax.fori_loop(0, nz, forward, (zero,) * (6 * half), unroll=5)
+                    new[i] = p * inv - low * new[i]
+                    vf[k, ch, at, :] = new[i]
+            return tuple(new)
+
+        carry = (zero,) * (4 * half)
+        for j, (at, size) in enumerate(parts):
+            carry = lax.fori_loop(at, at + size, forward, carry, unroll=5)
+            if j == 0:
+                relay(lats, 2)
 
         copies = [pltpu.make_async_copy(pb.at[:, :, 0, :], pe.at[:, 0:4, :], dsem.at[0]),
                   pltpu.make_async_copy(pb.at[:, :, rows - 1, :], pe.at[:, 4:8, :], dsem.at[1])]
@@ -312,9 +378,8 @@
             w15 = jnp.where(wet, F32(SPR), 0.0)
             grad = grad + push * jnp.where(wet, 0.75 * salt - 0.25 * warm, 0.0)
             p = pe[k] + ((w15 + slope * vel) * (sign * g) - w15 * centre[k]) + grad
-            depth = dce[...]
-            inv = jnp.where((k + 1) == depth, tab[1, k], tab[0, k])
-            prev = jnp.where(k < depth, (p - MIX * prev) * inv, 0.0)
+            inv = inverse(k, dce[...])
+            prev = p * inv - (MIX * inv) * prev
             ve[k] = prev
             return prev, grad
 
@@ -328,10 +393,15 @@
 
         lax.fori_loop(0, nz, backward, zero, unroll=25)
 
+    depth_maps()
+    relay(lat_depth, 0)
+    stencil(st1, True)
+    relay(lat_1, 0)
     for one in lon_1:
         one.wait_recv()
-    depth_maps()
-    main(st1, 0, st2, PAD)
+    columns(0)
+    relay(lat_1, 1)
+    sweeps(st2, PAD, lat_1)
 
     loads[2].wait()
     loads[3].wait()
@@ -348,9 +418,13 @@
     for one in patch:
         one.wait()
     lon_2 = send_lon(1, pack(st2, False))
+    stencil(st2, False)
+    relay(lat_2, 0)
     for one in lon_2:
         one.wait_recv()
-    main(st2, 1, out, 0)
+    columns(1)
+    relay(lat_2, 1)
+    sweeps(out, 0, lat_2)
     recv_lat(*lat_2)
     edges(g2, xe, xe2)
     last = [pltpu.make_async_copy(xe2.at[:, 0:4, :], out.at[:, :, 0, :], bsem.at[0]),
@@ -387,6 +461,9 @@
                 pltpu.VMEM((5, rows, cols), jnp.int32),
                 pltpu.VMEM((3, nz, 8, cols), F32),
                 edge, edge, edge, edge, edge, edge, edge,
+                pltpu.VMEM((nz, 4, cols), F32),
+                pltpu.VMEM((nz, 4, cols), F32),
+                pltpu.VMEM((1, cols), jnp.int32),
                 pltpu.VMEM((2, 1, cols), jnp.int32),
                 pltpu.VMEM((8, cols), jnp.int32),
                 pltpu.VMEM((8, cols), jnp.int32),
@@ -394,10 +471,11 @@
                 pltpu.VMEM((2, 4, rows, cols), F32),
                 pltpu.VMEM((2, 4, rows, cols), F32),
                 pltpu.VMEM((2, 4, rows, cols), F32),
-                dma((4,)), dma((8,)), dma((8,)), dma((4,)), dma((4,)), dma((2,)), dma((2,)),
+                pltpu.VMEM((2, 4, rows, cols), F32),
+                dma((4,)), dma((20,)), dma((20,)), dma((4,)), dma((4,)), dma((2,)), dma((2,)),
             ],
             compiler_params=pltpu.CompilerParams(
-                collective_id=0, has_side_effects=True, vmem_limit_bytes=48 << 20
+                collective_id=0, has_side_effects=True, vmem_limit_bytes=50 << 20
             ),
         )(state, depth_levels)
 

time: 33.8 us -> 30 us (0.89)
  the two profiles are of different devices: /device:TPU:16 before, /device:TPU:56 now
where the time goes in v2:
time: 30 us; the launch traced here: 29.9 us
  Pallas kernels  27.7 us (92%)
  local copies, waits for them, and re-layouts  2.14 us (7%)
    pallas_call x1, Pallas kernels, on_device(): pl.pallas_call(functools.partial(kernel, nlon, nlat, nz), out_shape=jax.S...  27.7 us
    unnamed x3, local copies, waits for them, and re-layouts  2.14 us

profile of v2, /device:TPU:56, one launch (start us, length us, event | category | flops | bytes accessed | tf_op | source)
XLA Modules:
  0.0 29.9 jit_solution(9396023082980888532)
XLA Ops:
  0.0 0.0 copy-start
  0.0 0.7 %copy-done = s32[16,128]{1,0:T(8,128)S(1)} copy-done((s32[16,128]{1,0:T(8,128)S(1)}, s32[16,128]{1,0:T(8,128)}, u32[]{:S(2)}) %copy-start) | copy-done | bytes 8216
  0.7 27.7 %shard_map.28 = f32[75,4,16,128]{3,2,1,0:T(8,128)S(1)} custom-call(f32[75,4,16,128]{3,2,1,0:T(8,128)} %x.1, s32[16,128]{1,0:T(8,128)S(1)} %copy-done), custom_call_target="tpu_custom_call" | custom-call | tf_op jit(solution)/shard_map/pallas_call | solution.py:450
  28.4 1.4 %copy.4 = f32[75,4,16,128]{3,2,1,0:T(8,128)} copy(f32[75,4,16,128]{3,2,1,0:T(8,128)S(1)} %shard_map.28) | data formatting | bytes 4915200
Async XLA Ops:
  0.0 0.7 %copy-start = (s32[16,128]{1,0:T(8,128)S(1)}, s32[16,128]{1,0:T(8,128)}, u32[]{:S(2)}) copy-start(s32[16,128]{1,0:T(8,128)} %dep.1) | copy-start | bytes 24580

commit v3 on v2

--- a/solution.py
+++ b/solution.py
@@ -13,12 +13,13 @@
 ADV = 0.25
 SPR = 0.15
 PAD = 8
+PARTS = 5
 
 
 def kernel(nlon, nlat, nz, x, dep, out,
            st1, st2, vf, pb, dpad, dm, tab,
            xc, g1, g2, pe, ve, xe, xe2, h1, h2, hd, gd, dge, dce,
-           cw, ce, hw, he, ca,
+           cw, ce, hw, he, ca, cx,
            lsem, ssem, rsem, csem, crsem, dsem, bsem):
     rows = x.shape[2]
     half = rows // 8
@@ -58,13 +59,15 @@
     def load(i, src, dst):
         return pltpu.make_async_copy(src, dst, lsem.at[i])
 
+    size = nz // PARTS
+    parts = [(j * size, size if j < PARTS - 1 else nz - j * size) for j in range(PARTS)]
     loads = [
-        load(0, x, st1.at[:, :, PAD:PAD + rows, :]),
-        load(1, dep, dpad.at[PAD:PAD + rows, :]),
-        load(2, x.at[:, :, 0, :], xc.at[:, 0:4, :]),
-        load(3, x.at[:, :, rows - 1, :], xc.at[:, 4:8, :]),
+        load(0, dep, dpad.at[PAD:PAD + rows, :]),
+        load(1, x.at[:, :, 0, :], xc.at[:, 0:4, :]),
+        load(2, x.at[:, :, rows - 1, :], xc.at[:, 4:8, :]),
     ]
-    for one in loads:
+    body_loads = [load(3 + j, x.at[pl.ds(at, n)], st1.at[pl.ds(at, n), :, PAD:PAD + rows, :]) for j, (at, n) in enumerate(parts)]
+    for one in loads[0:1] + body_loads + loads[1:3]:
         one.start()
 
     @pl.when(bottom)
@@ -79,40 +82,44 @@
     def _():
         pl.semaphore_wait(barrier, 4)
 
-    def along_lat(base, south_row, north_row, ghost, held, parts):
+    def along_lat(base, south_row, north_row, ghost, held, pieces):
         def copy(src, dst, i, device):
             return pltpu.make_async_remote_copy(src, dst, ssem.at[i], rsem.at[i], device_id=device, device_id_type=MESH)
 
-        up = copy(north_row, ghost(0), base, north)
-        down = copy(south_row, ghost(1), base + 1, south)
-        over, on = [], []
-        for j, (at, size) in enumerate(parts):
-            part = pl.ds(at, size)
-            over.append(copy(north_row.at[part], held.at[part], base + 2 + 2 * j, over_south))
-            on.append(copy(held.at[part], ghost(1).at[part], base + 3 + 2 * j, north))
-        return up, down, over, on
-
-    def start_lat(up, down, over, on):
-        @pl.when(top)
-        def _():
-            for one in over:
-                one.start()
-
-        @pl.when(jnp.logical_not(top))
-        def _():
-            up.start()
-
-        @pl.when(jnp.logical_not(bottom))
-        def _():
-            down.start()
+        out = []
+        for j, (at, n) in enumerate(pieces):
+            part, i = pl.ds(at, n), base + 4 * j
+            out.append((
+                copy(north_row.at[part], ghost(0).at[part], i, north),
+                copy(south_row.at[part], ghost(1).at[part], i + 1, south),
+                copy(north_row.at[part], held.at[part], i + 2, over_south),
+                copy(held.at[part], ghost(1).at[part], i + 3, north),
+            ))
+        return out
+
+    def start_lat(lats):
+        for up, down, over, on in lats:
+            @pl.when(top)
+            def _():
+                over.start()
+
+            @pl.when(jnp.logical_not(top))
+            def _():
+                up.start()
+
+            @pl.when(jnp.logical_not(bottom))
+            def _():
+                down.start()
 
     def relay(lats, j):
         @pl.when(near)
         def _():
-            lats[2][j].wait_recv()
-            lats[3][j].start()
-
-    def recv_lat(up, down, over, on):
+            lats[j][2].wait_recv()
+            lats[j][3].start()
+
+    def recv_lat(lats, j):
+        up, down, over, on = lats[j]
+
         @pl.when(jnp.logical_not(bottom))
         def _():
             up.wait_recv()
@@ -123,38 +130,34 @@
 
         @pl.when(top)
         def _():
-            for one in on:
-                one.wait_recv()
-
-    def sent_lat(up, down, over, on):
-        @pl.when(jnp.logical_not(top))
-        def _():
-            up.wait_send()
-
-        @pl.when(top)
-        def _():
-            for one in over:
-                one.wait_send()
-
-        @pl.when(near)
-        def _():
-            for one in on:
-                one.wait_send()
-
-        @pl.when(jnp.logical_not(bottom))
-        def _():
-            down.wait_send()
+            on.wait_recv()
+
+    def sent_lat(lats):
+        for up, down, over, on in lats:
+            @pl.when(jnp.logical_not(top))
+            def _():
+                up.wait_send()
+
+            @pl.when(top)
+            def _():
+                over.wait_send()
+
+            @pl.when(near)
+            def _():
+                on.wait_send()
+
+            @pl.when(jnp.logical_not(bottom))
+            def _():
+                down.wait_send()
 
     def ghost_in(buf):
         return lambda e: buf.at[:, 4 * e:4 * e + 4, :]
 
-    third = nz // 3
-    parts = [(0, third), (third, third), (2 * third, nz - 2 * third)]
     lat_depth = along_lat(0, dep.at[0:1, :], dep.at[rows - 1:rows, :], lambda e: gd.at[e], hd, [(0, 1)])
     lat_1 = along_lat(4, x.at[:, :, 0, :], x.at[:, :, rows - 1, :], ghost_in(g1), h1, parts)
-    lat_2 = along_lat(12, xe.at[:, 0:4, :], xe.at[:, 4:8, :], ghost_in(g2), h2, parts)
-    start_lat(*lat_depth)
-    start_lat(*lat_1)
+    lat_2 = along_lat(4 + 4 * PARTS, xe.at[:, 0:4, :], xe.at[:, 4:8, :], ghost_in(g2), h2, parts)
+    start_lat(lat_depth)
+    start_lat(lat_1)
 
     zero = jnp.zeros((8, 128), F32)
 
@@ -178,26 +181,34 @@
 
     lax.fori_loop(0, nz, clear_pads, 0, unroll=5)
 
-    def pack(st, depth_too):
+    def collect(acc, i, j, value, k):
+        v = pltpu.roll(value, k + 1, 1)
+        acc[i] = jnp.where(lane == k + 1, v, acc[i])
+        acc[j] = jnp.where(lane == k, v, acc[j])
+
+    def collected(acc):
+        n = len(acc) // 2
+        return [pltpu.roll(v, 127, 1) if i < n else v for i, v in enumerate(acc)]
+
+    def pack(st, waits):
         def body(k, acc):
             acc = list(acc)
-            here = lane == k
             for ch in range(4):
                 for h in range(half):
-                    v = st[k, ch, pl.ds(PAD + 8 * h, 8), :]
                     i = ch * half + h
-                    acc[i] = jnp.where(here, pltpu.roll(v, k, 1), acc[i])
-                    i += 4 * half
-                    acc[i] = jnp.where(here, pltpu.roll(v, k + 1, 1), acc[i])
+                    collect(acc, i, 4 * half + i, st[k, ch, pl.ds(PAD + 8 * h, 8), :], k)
             return tuple(acc)
 
-        acc = list(lax.fori_loop(0, nz, body, (zero,) * (8 * half), unroll=15))
-        if depth_too:
-            for h in range(half):
-                d = dpad[pl.ds(PAD + 8 * h, 8), :].astype(F32)
-                acc[h] = jnp.where(lane == nz, pltpu.roll(d, nz, 1), acc[h])
-                i = 4 * half + h
-                acc[i] = jnp.where(lane == nz, pltpu.roll(d, nz + 1, 1), acc[i])
+        acc = (zero,) * (8 * half)
+        for j, (at, n) in enumerate(parts):
+            waits[j].wait()
+            acc = lax.fori_loop(at, at + n, body, acc, unroll=15)
+        acc = collected(acc)
+        for h in range(half):
+            d = dpad[pl.ds(PAD + 8 * h, 8), :].astype(F32)
+            acc[h] = jnp.where(lane == nz, pltpu.roll(d, nz, 1), acc[h])
+            i = 4 * half + h
+            acc[i] = jnp.where(lane == nz, pltpu.roll(d, nz + 1, 1), acc[i])
         return acc
 
     def lon_copies(step):
@@ -206,22 +217,25 @@
 
         return [copy(cw.at[step], he.at[step], 0, west), copy(ce.at[step], hw.at[step], 1, east)]
 
-    def send_lon(step, acc):
+    def send_lon(step, acc, ends):
         for ch in range(4):
             for h in range(half):
                 i = ch * half + h
                 cw[step, ch, pl.ds(8 * h, 8), :] = acc[i]
                 ce[step, ch, pl.ds(8 * h, 8), :] = acc[4 * half + i]
+        for buf, end in zip((cw, ce), ends):
+            for ch in range(4):
+                buf[step, ch, 0:1, :] = end[ch:ch + 1]
+                buf[step, ch, rows - 1:rows, :] = end[4 + ch:5 + ch]
         copies = lon_copies(step)
         for one in copies:
             one.start()
         return copies
 
-    loads[1].wait()
+    loads[0].wait()
     dpad[0:PAD, :] = jnp.zeros((8, 128), jnp.int32)
     dpad[PAD + rows:PAD + rows + 8, :] = jnp.zeros((8, 128), jnp.int32)
-    loads[0].wait()
-    lon_1 = send_lon(0, pack(st1, True))
+    lon_1 = send_lon(0, pack(st1, body_loads), [])
 
     first, final = lane == 0, lane == 127
 
@@ -242,9 +256,11 @@
         return 0.1 + 0.4 * (row + 0.5) / total
 
     def dense(warm, salt, wet):
-        return jnp.where(wet, 0.75 * salt - 0.25 * warm, 0.0)
-
-    def stencil(st, make_table):
+        return jnp.where(wet, 0.075 * salt - 0.025 * warm, 0.0)
+
+    def stencil(st, make_table, lats):
+        turns = [rotation(h) for h in range(half)]
+
         def body(k, carry):
             grad_e = list(carry[0:half])
             grad_n = list(carry[half:2 * half])
@@ -272,17 +288,25 @@
                 centre = 1.0 - (w15[0] + w15[1]) - (w15[2] + w15[3])
                 grad_e[h] = grad_e[h] + (dense(qe[0], qe[1], wet[1]) - dense(qw[0], qw[1], wet[2]))
                 grad_n[h] = grad_n[h] + (dense(qn[0], qn[1], wet[3]) - dense(qs[0], qs[1], wet[4]))
-                turn = rotation(h)
+                turn = turns[h]
                 for ch in range(4):
                     p = (centre * q[ch] + a_e * qe[ch]) + (a_w * qw[ch] + a_n * qn[ch]) + a_s * qs[ch]
                     if ch == 2:
-                        p = p + (turn * q[3] - 0.1 * grad_e[h])
+                        p = p + (turn * q[3] - grad_e[h])
                     if ch == 3:
-                        p = p - (turn * q[2] + 0.1 * grad_n[h])
+                        p = p - (turn * q[2] + grad_n[h])
                     pb[k, ch, at, :] = p
             return tuple(grad_e + grad_n + [upper])
 
-        lax.fori_loop(0, nz, body, (zero,) * (2 * half + 1), unroll=5)
+        carry = (zero,) * (2 * half + 1)
+        for j, (at, n) in enumerate(parts):
+            carry = lax.fori_loop(at, at + n, body, carry, unroll=5)
+            relay(lats, j)
+        copies = [pltpu.make_async_copy(pb.at[:, :, 0, :], pe.at[:, 0:4, :], dsem.at[0]),
+                  pltpu.make_async_copy(pb.at[:, :, rows - 1, :], pe.at[:, 4:8, :], dsem.at[1])]
+        for one in copies:
+            one.start()
+        return copies
 
     def columns(step):
         for h in range(half):
@@ -300,13 +324,17 @@
                     push = push + jnp.where(lane >= shift, pltpu.roll(push, shift, 1), 0.0)
                     shift *= 2
                 add = [coef * q[ch] - w15 * own[step, ch, at, :] for ch in range(4)]
-                add[2] = add[2] + (way * 0.1) * push
+                add[2] = add[2] + way * push
                 adds.append(add)
             even = lax.rem(lane, 2) == 0
             for ch in range(4):
                 w, e = adds[0][ch], pltpu.roll(adds[1][ch], 127, 1)
                 ca[0, ch, at, :] = jnp.where(even, w, e)
                 ca[1, ch, at, :] = jnp.where(even, e, w)
+        for odd in range(2):
+            for ch in range(4):
+                cx[odd, ch:ch + 1, :] = ca[odd, ch, 0:1, :]
+                cx[odd, 4 + ch:5 + ch, :] = ca[odd, ch, rows - 1:rows, :]
 
     outer = jnp.logical_or(first, final)
 
@@ -314,7 +342,7 @@
         inv = jnp.where((k + 1) == depth, tab[1, k], tab[0, k])
         return jnp.where(k < depth, inv, 0.0)
 
-    def sweeps(dst, dst_row, lats):
+    def sweeps(dst, dst_row, gather):
         def forward(k, carry):
             new = list(carry)
             back = lax.rem(128 - k, 128)
@@ -325,48 +353,41 @@
                 low = MIX * inv
                 for ch in range(4):
                     p = pb[k, ch, at, :] + jnp.where(outer, pltpu.roll(ca[odd, ch, at, :], back, 1), 0.0)
-                    pb[k, ch, at, :] = p
                     i = ch * half + h
                     new[i] = p * inv - low * new[i]
                     vf[k, ch, at, :] = new[i]
             return tuple(new)
 
-        carry = (zero,) * (4 * half)
-        for j, (at, size) in enumerate(parts):
-            carry = lax.fori_loop(at, at + size, forward, carry, unroll=5)
-            if j == 0:
-                relay(lats, 2)
-
-        copies = [pltpu.make_async_copy(pb.at[:, :, 0, :], pe.at[:, 0:4, :], dsem.at[0]),
-                  pltpu.make_async_copy(pb.at[:, :, rows - 1, :], pe.at[:, 4:8, :], dsem.at[1])]
-        for one in copies:
-            one.start()
+        lax.fori_loop(0, nz, forward, (zero,) * (4 * half), unroll=15)
 
         def backward(j, carry):
             k = nz - 1 - j
             up = tab[2, k]
-            new = []
+            new = list(carry)
             for ch in range(4):
                 for h in range(half):
-                    s = vf[k, ch, pl.ds(8 * h, 8), :] - up * carry[ch * half + h]
+                    i = ch * half + h
+                    s = vf[k, ch, pl.ds(8 * h, 8), :] - up * carry[i]
                     dst[k, ch, pl.ds(dst_row + 8 * h, 8), :] = s
-                    new.append(s)
+                    new[i] = s
+                    if gather:
+                        collect(new, 4 * half + i, 8 * half + i, s, k)
             return tuple(new)
 
-        lax.fori_loop(0, nz, backward, (zero,) * (4 * half), unroll=15)
-        for one in copies:
-            one.wait()
+        count = (12 if gather else 4) * half
+        carry = lax.fori_loop(0, nz, backward, (zero,) * count, unroll=15)
+        return collected(carry[4 * half:])
 
     flip = jnp.logical_and(top, sub >= 4)
     index = jnp.where(flip, 127 - lane, lane)
     sign = jnp.where(jnp.logical_and(flip, lax.rem(sub, 4) >= 2), F32(-1.0), F32(1.0))
     slope = jnp.where(lo, F32(ADV), jnp.where(top, F32(ADV), F32(-ADV)))
-    push = jnp.where(sub == 3, F32(0.1), jnp.where(sub == 7, F32(-0.1), F32(0.0)))
+    push = jnp.where(sub == 3, F32(1.0), jnp.where(sub == 7, F32(-1.0), F32(0.0)))
 
     def mirrored(v):
         return jnp.take_along_axis(v, index, axis=1)
 
-    def edges(ghost, centre, solved):
+    def edges(ghost, centre, solved, lats, gather):
         def both(k, c):
             return mirrored(jnp.where(lo, ghost[k, c:c + 1, :], ghost[k, c + 4:c + 5, :]))
 
@@ -376,66 +397,68 @@
             warm, salt, vel = both(k, 0), both(k, 1), both(k, 3)
             wet = k < dge[...]
             w15 = jnp.where(wet, F32(SPR), 0.0)
-            grad = grad + push * jnp.where(wet, 0.75 * salt - 0.25 * warm, 0.0)
-            p = pe[k] + ((w15 + slope * vel) * (sign * g) - w15 * centre[k]) + grad
+            grad = grad + push * dense(warm, salt, wet)
+            side = jnp.where(outer, pltpu.roll(cx[lax.rem(k, 2)], lax.rem(128 - k, 128), 1), 0.0)
+            p = (pe[k] + side) + ((w15 + slope * vel) * (sign * g) - w15 * centre[k]) + grad
             inv = inverse(k, dce[...])
             prev = p * inv - (MIX * inv) * prev
             ve[k] = prev
             return prev, grad
 
-        lax.fori_loop(0, nz, forward, (zero, zero), unroll=25)
-
-        def backward(j, s):
+        carry = (zero, zero)
+        for j, (at, n) in enumerate(parts):
+            recv_lat(lats, j)
+            carry = lax.fori_loop(at, at + n, forward, carry, unroll=15)
+
+        def backward(j, carry):
             k = nz - 1 - j
-            s = ve[k] - tab[2, k] * s
-            solved[k] = s
-            return s
-
-        lax.fori_loop(0, nz, backward, zero, unroll=25)
+            new = list(carry)
+            new[0] = ve[k] - tab[2, k] * carry[0]
+            solved[k] = new[0]
+            if gather:
+                collect(new, 1, 2, new[0], k)
+            return tuple(new)
+
+        carry = lax.fori_loop(0, nz, backward, (zero,) * (3 if gather else 1), unroll=25)
+        return collected(carry[1:])
 
     depth_maps()
     relay(lat_depth, 0)
-    stencil(st1, True)
-    relay(lat_1, 0)
+    copies = stencil(st1, True, lat_1)
     for one in lon_1:
         one.wait_recv()
     columns(0)
-    relay(lat_1, 1)
-    sweeps(st2, PAD, lat_1)
-
-    loads[2].wait()
-    loads[3].wait()
-    recv_lat(*lat_depth)
+    for one in copies + loads[1:3]:
+        one.wait()
+    recv_lat(lat_depth, 0)
     dce[...] = jnp.where(lo, dm[0, 0:1, :], dm[0, rows - 1:rows, :])
     dge[...] = mirrored(jnp.where(lo, gd[0], gd[1]).astype(F32)).astype(jnp.int32)
-    recv_lat(*lat_1)
-    edges(g1, xc, xe)
-    start_lat(*lat_2)
+    ends = edges(g1, xc, xe, lat_1, True)
+    start_lat(lat_2)
+    lon_2 = send_lon(1, sweeps(st2, PAD, True), ends)
     patch = [pltpu.make_async_copy(xe.at[:, 0:4, :], st2.at[:, :, PAD, :], bsem.at[0]),
              pltpu.make_async_copy(xe.at[:, 4:8, :], st2.at[:, :, PAD + rows - 1, :], bsem.at[1])]
     for one in patch:
         one.start()
     for one in patch:
         one.wait()
-    lon_2 = send_lon(1, pack(st2, False))
-    stencil(st2, False)
-    relay(lat_2, 0)
+    copies = stencil(st2, False, lat_2)
     for one in lon_2:
         one.wait_recv()
     columns(1)
-    relay(lat_2, 1)
-    sweeps(out, 0, lat_2)
-    recv_lat(*lat_2)
-    edges(g2, xe, xe2)
+    sweeps(out, 0, False)
+    for one in copies:
+        one.wait()
+    edges(g2, xe, xe2, lat_2, False)
     last = [pltpu.make_async_copy(xe2.at[:, 0:4, :], out.at[:, :, 0, :], bsem.at[0]),
             pltpu.make_async_copy(xe2.at[:, 4:8, :], out.at[:, :, rows - 1, :], bsem.at[1])]
     for one in last:
         one.start()
     for one in lon_1 + lon_2:
         one.wait_send()
-    sent_lat(*lat_depth)
-    sent_lat(*lat_1)
-    sent_lat(*lat_2)
+    sent_lat(lat_depth)
+    sent_lat(lat_1)
+    sent_lat(lat_2)
     for one in last:
         one.wait()
 
@@ -472,7 +495,8 @@
                 pltpu.VMEM((2, 4, rows, cols), F32),
                 pltpu.VMEM((2, 4, rows, cols), F32),
                 pltpu.VMEM((2, 4, rows, cols), F32),
-                dma((4,)), dma((20,)), dma((20,)), dma((4,)), dma((4,)), dma((2,)), dma((2,)),
+                pltpu.VMEM((2, 8, cols), F32),
+                dma((3 + PARTS,)), dma((4 + 8 * PARTS,)), dma((4 + 8 * PARTS,)), dma((4,)), dma((4,)), dma((2,)), dma((2,)),
             ],
             compiler_params=pltpu.CompilerParams(
                 collective_id=0, has_side_effects=True, vmem_limit_bytes=50 << 20

time: 30 us -> 28.8 us (0.960)
  the two profiles are of different devices: /device:TPU:56 before, /device:TPU:25 now
where the time goes in v3:
time: 28.8 us; the launch traced here: 28.7 us
  Pallas kernels  26.5 us (92%)
  local copies, waits for them, and re-layouts  2.14 us (7%)
    pallas_call x1, Pallas kernels, on_device(): pl.pallas_call(functools.partial(kernel, nlon, nlat, nz), out_shape=jax.S...  26.5 us
    unnamed x3, local copies, waits for them, and re-layouts  2.14 us

profile of v3, /device:TPU:25, one launch (start us, length us, event | category | flops | bytes accessed | tf_op | source)
XLA Modules:
  0.0 28.7 jit_solution(11828523015680780929)
XLA Ops:
  0.0 0.0 copy-start
  0.0 0.7 %copy-done = s32[16,128]{1,0:T(8,128)S(1)} copy-done((s32[16,128]{1,0:T(8,128)S(1)}, s32[16,128]{1,0:T(8,128)}, u32[]{:S(2)}) %copy-start) | copy-done | bytes 8216
  0.7 26.5 %shard_map.28 = f32[75,4,16,128]{3,2,1,0:T(8,128)S(1)} custom-call(f32[75,4,16,128]{3,2,1,0:T(8,128)} %x.1, s32[16,128]{1,0:T(8,128)S(1)} %copy-done), custom_call_target="tpu_custom_call" | custom-call | tf_op jit(solution)/shard_map/pallas_call | solution.py:473
  27.2 1.4 %copy.4 = f32[75,4,16,128]{3,2,1,0:T(8,128)} copy(f32[75,4,16,128]{3,2,1,0:T(8,128)S(1)} %shard_map.28) | data formatting | bytes 4915200
Async XLA Ops:
  0.0 0.7 %copy-start = (s32[16,128]{1,0:T(8,128)S(1)}, s32[16,128]{1,0:T(8,128)}, u32[]{:S(2)}) copy-start(s32[16,128]{1,0:T(8,128)} %dep.1) | copy-start | bytes 24580

commit v4 on v3

--- a/solution.py
+++ b/solution.py
@@ -161,26 +161,6 @@
 
     zero = jnp.zeros((8, 128), F32)
 
-    @pl.when(bottom)
-    def _():
-        gd[0] = jnp.zeros_like(gd[0])
-
-        def clear(k, c):
-            g1[k, 0:4] = zero[0:4]
-            g2[k, 0:4] = zero[0:4]
-            return c
-
-        lax.fori_loop(0, nz, clear, 0, unroll=5)
-
-    def clear_pads(k, c):
-        for ch in range(4):
-            for st in (st1, st2):
-                st[k, ch, 0:PAD, :] = zero
-                st[k, ch, PAD + rows:PAD + rows + 8, :] = zero
-        return c
-
-    lax.fori_loop(0, nz, clear_pads, 0, unroll=5)
-
     def collect(acc, i, j, value, k):
         v = pltpu.roll(value, k + 1, 1)
         acc[i] = jnp.where(lane == k + 1, v, acc[i])
@@ -236,6 +216,26 @@
     dpad[0:PAD, :] = jnp.zeros((8, 128), jnp.int32)
     dpad[PAD + rows:PAD + rows + 8, :] = jnp.zeros((8, 128), jnp.int32)
     lon_1 = send_lon(0, pack(st1, body_loads), [])
+
+    @pl.when(bottom)
+    def _():
+        gd[0] = jnp.zeros_like(gd[0])
+
+        def clear(k, c):
+            g1[k, 0:4] = zero[0:4]
+            g2[k, 0:4] = zero[0:4]
+            return c
+
+        lax.fori_loop(0, nz, clear, 0, unroll=5)
+
+    def clear_pads(k, c):
+        for ch in range(4):
+            for st in (st1, st2):
+                st[k, ch, 0:PAD, :] = zero
+                st[k, ch, PAD + rows:PAD + rows + 8, :] = zero
+        return c
+
+    lax.fori_loop(0, nz, clear_pads, 0, unroll=5)
 
     first, final = lane == 0, lane == 127
 
@@ -387,7 +387,7 @@
     def mirrored(v):
         return jnp.take_along_axis(v, index, axis=1)
 
-    def edges(ghost, centre, solved, lats, gather):
+    def edges(ghost, centre, solved, lats, gather, into=None):
         def both(k, c):
             return mirrored(jnp.where(lo, ghost[k, c:c + 1, :], ghost[k, c + 4:c + 5, :]))
 
@@ -415,6 +415,10 @@
             new = list(carry)
             new[0] = ve[k] - tab[2, k] * carry[0]
             solved[k] = new[0]
+            if into is not None:
+                for ch in range(4):
+                    into[k, ch, 0:1, :] = new[0][ch:ch + 1]
+                    into[k, ch, rows - 1:rows, :] = new[0][4 + ch:5 + ch]
             if gather:
                 collect(new, 1, 2, new[0], k)
             return tuple(new)
@@ -449,18 +453,12 @@
     sweeps(out, 0, False)
     for one in copies:
         one.wait()
-    edges(g2, xe, xe2, lat_2, False)
-    last = [pltpu.make_async_copy(xe2.at[:, 0:4, :], out.at[:, :, 0, :], bsem.at[0]),
-            pltpu.make_async_copy(xe2.at[:, 4:8, :], out.at[:, :, rows - 1, :], bsem.at[1])]
-    for one in last:
-        one.start()
+    edges(g2, xe, xe2, lat_2, False, out)
     for one in lon_1 + lon_2:
         one.wait_send()
     sent_lat(lat_depth)
     sent_lat(lat_1)
     sent_lat(lat_2)
-    for one in last:
-        one.wait()
 
 
 def solution(mesh):
@@ -501,7 +499,7 @@
             compiler_params=pltpu.CompilerParams(
                 collective_id=0, has_side_effects=True, vmem_limit_bytes=50 << 20
             ),
-        )(state, depth_levels)
+        )(state, pltpu.with_memory_space_constraint(depth_levels, pltpu.HBM))
 
     return jax.shard_map(
         on_device,

time: 28.8 us -> 28 us (0.972)
  local copies, waits for them, and re-layouts: 2.14 us -> 1.44 us
    unnamed x3 -> x1, local copies, waits for them, and re-layouts: 2.14 us -> 1.44 us
where the time goes in v4:
time: 28 us; the launch traced here: 27.9 us
  Pallas kernels  26.4 us (94%)
  local copies, waits for them, and re-layouts  1.44 us (5%)
    pallas_call x1, Pallas kernels, on_device(): pl.pallas_call(functools.partial(kernel, nlon, nlat, nz), out_shape=jax.S...  26.4 us
    unnamed x1, local copies, waits for them, and re-layouts  1.44 us

profile of v4, /device:TPU:25, one launch (start us, length us, event | category | flops | bytes accessed | tf_op | source)
XLA Modules:
  0.0 27.9 jit_solution(90578834600553243)
XLA Ops:
  0.0 26.4 %shard_map.28 = f32[75,4,16,128]{3,2,1,0:T(8,128)S(1)} custom-call(f32[75,4,16,128]{3,2,1,0:T(8,128)} %x.1, s32[16,128]{1,0:T(8,128)} %dep.1), custom_call_target="tpu_custom_call" | custom-call | tf_op jit(solution)/shard_map/pallas_call | solution.py:471
  26.4 1.4 %copy.4 = f32[75,4,16,128]{3,2,1,0:T(8,128)} copy(f32[75,4,16,128]{3,2,1,0:T(8,128)S(1)} %shard_map.28) | data formatting | bytes 4915200

commit v5 on v4

--- a/solution.py
+++ b/solution.py
@@ -19,7 +19,7 @@
 def kernel(nlon, nlat, nz, x, dep, out,
            st1, st2, vf, pb, dpad, dm, tab,
            xc, g1, g2, pe, ve, xe, xe2, h1, h2, hd, gd, dge, dce,
-           cw, ce, hw, he, ca, cx,
+           cw, ce, hw, he, ca, cx, cp,
            lsem, ssem, rsem, csem, crsem, dsem, bsem):
     rows = x.shape[2]
     half = rows // 8
@@ -319,15 +319,10 @@
                 q = [halo[step, ch, at, :] for ch in range(4)]
                 coef = w15 + (way * ADV) * q[2]
                 push = dense(q[0], q[1], wet)
-                shift = 1
-                while shift < nz:
-                    push = push + jnp.where(lane >= shift, pltpu.roll(push, shift, 1), 0.0)
-                    shift *= 2
                 add = [coef * q[ch] - w15 * own[step, ch, at, :] for ch in range(4)]
-                add[2] = add[2] + way * push
-                adds.append(add)
+                adds.append(add + [way * push])
             even = lax.rem(lane, 2) == 0
-            for ch in range(4):
+            for ch in range(5):
                 w, e = adds[0][ch], pltpu.roll(adds[1][ch], 127, 1)
                 ca[0, ch, at, :] = jnp.where(even, w, e)
                 ca[1, ch, at, :] = jnp.where(even, e, w)
@@ -335,6 +330,7 @@
             for ch in range(4):
                 cx[odd, ch:ch + 1, :] = ca[odd, ch, 0:1, :]
                 cx[odd, 4 + ch:5 + ch, :] = ca[odd, ch, rows - 1:rows, :]
+            cp[odd] = jnp.where(lo, ca[odd, 4, 0:1, :], ca[odd, 4, rows - 1:rows, :])
 
     outer = jnp.logical_or(first, final)
 
@@ -351,14 +347,19 @@
                 at = pl.ds(8 * h, 8)
                 inv = inverse(k, dm[0, at, :])
                 low = MIX * inv
+                j = 4 * half + h
+                new[j] = new[j] + pltpu.roll(ca[odd, 4, at, :], back, 1)
                 for ch in range(4):
-                    p = pb[k, ch, at, :] + jnp.where(outer, pltpu.roll(ca[odd, ch, at, :], back, 1), 0.0)
+                    side = pltpu.roll(ca[odd, ch, at, :], back, 1)
+                    if ch == 2:
+                        side = side + new[j]
+                    p = pb[k, ch, at, :] + jnp.where(outer, side, 0.0)
                     i = ch * half + h
                     new[i] = p * inv - low * new[i]
                     vf[k, ch, at, :] = new[i]
             return tuple(new)
 
-        lax.fori_loop(0, nz, forward, (zero,) * (4 * half), unroll=15)
+        lax.fori_loop(0, nz, forward, (zero,) * (5 * half), unroll=15)
 
         def backward(j, carry):
             k = nz - 1 - j
@@ -387,25 +388,30 @@
     def mirrored(v):
         return jnp.take_along_axis(v, index, axis=1)
 
+    eastward = lax.rem(sub, 4) == 2
+
     def edges(ghost, centre, solved, lats, gather, into=None):
         def both(k, c):
             return mirrored(jnp.where(lo, ghost[k, c:c + 1, :], ghost[k, c + 4:c + 5, :]))
 
         def forward(k, carry):
-            prev, grad = carry
+            prev, grad, flank = carry
+            odd, back = lax.rem(k, 2), lax.rem(128 - k, 128)
+            flank = flank + pltpu.roll(cp[odd], back, 1)
             g = mirrored(ghost[k])
             warm, salt, vel = both(k, 0), both(k, 1), both(k, 3)
             wet = k < dge[...]
             w15 = jnp.where(wet, F32(SPR), 0.0)
             grad = grad + push * dense(warm, salt, wet)
-            side = jnp.where(outer, pltpu.roll(cx[lax.rem(k, 2)], lax.rem(128 - k, 128), 1), 0.0)
+            side = pltpu.roll(cx[odd], back, 1) + jnp.where(eastward, flank, 0.0)
+            side = jnp.where(outer, side, 0.0)
             p = (pe[k] + side) + ((w15 + slope * vel) * (sign * g) - w15 * centre[k]) + grad
             inv = inverse(k, dce[...])
             prev = p * inv - (MIX * inv) * prev
             ve[k] = prev
-            return prev, grad
-
-        carry = (zero, zero)
+            return prev, grad, flank
+
+        carry = (zero, zero, zero)
         for j, (at, n) in enumerate(parts):
             recv_lat(lats, j)
             carry = lax.fori_loop(at, at + n, forward, carry, unroll=15)
@@ -492,7 +498,8 @@
                 pltpu.VMEM((2, 4, rows, cols), F32),
                 pltpu.VMEM((2, 4, rows, cols), F32),
                 pltpu.VMEM((2, 4, rows, cols), F32),
-                pltpu.VMEM((2, 4, rows, cols), F32),
+                pltpu.VMEM((2, 5, rows, cols), F32),
+                pltpu.VMEM((2, 8, cols), F32),
                 pltpu.VMEM((2, 8, cols), F32),
                 dma((3 + PARTS,)), dma((4 + 8 * PARTS,)), dma((4 + 8 * PARTS,)), dma((4,)), dma((4,)), dma((2,)), dma((2,)),
             ],

time: 28 us -> 27.8 us (level)
  no operation moved by 1% of the time
where the time goes in v5:
time: 27.8 us; the launch traced here: 27.6 us
  Pallas kernels  26.2 us (94%)
  local copies, waits for them, and re-layouts  1.44 us (5%)
    pallas_call x1, Pallas kernels, on_device(): pl.pallas_call(functools.partial(kernel, nlon, nlat, nz), out_shape=jax.S...  26.2 us
    unnamed x1, local copies, waits for them, and re-layouts  1.44 us

profile of v5, /device:TPU:25, one launch (start us, length us, event | category | flops | bytes accessed | tf_op | source)
XLA Modules:
  0.0 27.6 jit_solution(12465476287225999000)
XLA Ops:
  0.0 26.2 %shard_map.28 = f32[75,4,16,128]{3,2,1,0:T(8,128)S(1)} custom-call(f32[75,4,16,128]{3,2,1,0:T(8,128)} %x.1, s32[16,128]{1,0:T(8,128)} %dep.1), custom_call_target="tpu_custom_call" | custom-call | tf_op jit(solution)/shard_map/pallas_call | solution.py:477
  26.2 1.4 %copy.4 = f32[75,4,16,128]{3,2,1,0:T(8,128)} copy(f32[75,4,16,128]{3,2,1,0:T(8,128)S(1)} %shard_map.28) | data formatting | bytes 4915200
